TPU v7x, 256 devices: a whole 4x4x8 slice. The times are simulated.
256 devices in a mesh: band: 64 (over z, y, x_lo), slab: 4 (over x_hi, core).
Axes of the slice: x: 4 (x_hi: 2, x_lo: 2; x = x_hi * 2 + x_lo), y: 4, z: 8, core: 2. Of those that a mesh axis runs over, the one named last changes fastest.
Arguments:
- bands: float32 [256, 32, 24, 128], P('band', 'slab'), may hold values from -8 to 8
- potential: float32 [32, 24, 128], P('slab'), may hold values from -1 to 0
Outputs:
- filtered: float32 [256, 32, 24, 128], P('band', 'slab')
- correlation: float32 [256, 256], P('band')
- projected: float32 [256, 256], P('band')
All inputs are finite; a program needn't handle non-finite values.
Results may differ from a plain program's by a relative error of at most 0.000092.
Values sent between devices are 32-bit elements; how exact they have to be, the bound alone decides.
No kernel may reach another device: no remote copies, remote signals or barrier semaphores. Data moves between devices by JAX's collectives and lax.ppermute only.
A program may use at most 128 MiB of HBM per device.

v0:
```python
import jax
import jax.numpy as jnp
from jax import lax
from jax.sharding import PartitionSpec as P

centre = 4.5
half = 3.5


def extended(block, sides, width):
    for axis, dim in sides:
        count = lax.axis_size(axis)
        forward = [(i, i + 1) for i in range(count - 1)]
        forward.append((count - 1, 0))
        backward = [(target, source) for source, target in forward]
        low = lax.ppermute(
            lax.slice_in_dim(block, block.shape[dim] - width, None, axis=dim), axis, forward
        )
        high = lax.ppermute(lax.slice_in_dim(block, 0, width, axis=dim), axis, backward)
        block = jnp.concatenate([low, block, high], axis=dim)
    return block


def hamiltonian(field, potential):
    padded = extended(field, (("slab", 1),), 2)
    middle = padded[:, 2:-2]
    lap = (
        -2.5 * middle
        + 4.0 / 3.0 * (padded[:, 1:-3] + padded[:, 3:-1])
        - 1.0 / 12.0 * (padded[:, :-4] + padded[:, 4:])
    )
    for axis in (2, 3):
        lap = lap - 2.5 * middle
        lap = lap + 4.0 / 3.0 * (jnp.roll(middle, 1, axis) + jnp.roll(middle, -1, axis))
        lap = lap - 1.0 / 12.0 * (jnp.roll(middle, 2, axis) + jnp.roll(middle, -2, axis))
    return -0.5 * lap + potential[None] * middle


def body(bands, potential):
    previous = bands
    current = (hamiltonian(bands, potential) - centre * bands) / half
    for step in range(3):
        following = 2.0 * (hamiltonian(current, potential) - centre * current) / half - previous
        previous, current = (current, following)
    image = hamiltonian(current, potential)
    local_bands = current.shape[0]
    volume = 1.0 / (current.shape[1] * lax.axis_size("slab") * current.shape[2] * current.shape[3])
    flat = current.reshape(local_bands, -1)
    himage = image.reshape(local_bands, -1)
    piece = lax.all_gather(current, "band", axis=0, tiled=True)
    others = piece.reshape(piece.shape[0], -1)
    gram_part = jnp.dot(
        flat, others.T, precision=lax.Precision.HIGHEST, preferred_element_type=jnp.float32
    )
    proj_part = jnp.dot(
        himage, others.T, precision=lax.Precision.HIGHEST, preferred_element_type=jnp.float32
    )
    gram_total, proj_total = lax.psum((gram_part, proj_part), "slab")
    return (current, gram_total * volume, proj_total * volume)


def solution(mesh):
    in_specs = (P("band", "slab", None, None), P("slab", None, None))
    out_specs = (P("band", "slab", None, None), P("band", None), P("band", None))
    return jax.shard_map(body, mesh=mesh, in_specs=in_specs, out_specs=out_specs, check_vma=False)
```

profile of v0, /device:TPU:8, one launch (start us, length us, event | category | flops | bytes accessed | tf_op | source)
XLA Modules:
  0.0 698.7 jit_solution(11574022964327537829)
XLA Ops:
  7.2 0.0 all-gather.2.cloned.1.call-start
  7.2 1.0 fusion.155
  8.2 0.1 collective-permute-start
  8.3 3.2 collective-permute-start.1
  11.6 1.3 fusion.163
  12.9 1.2 fusion.157
  14.1 1.2 fusion.159
  15.3 1.3 fusion.160
  16.6 1.3 fusion.161
  18.0 1.3 fusion.162
  19.3 1.0 fusion.158
  20.3 0.9 broadcast_multiply_fusion.1
  21.2 1.0 fusion.156
  22.2 1.1 constant_dynamic-update-slice_fusion
  23.3 1.8 broadcast_multiply_fusion
  25.1 0.2 fusion.146
  25.2 0.2 fusion.147
  25.4 0.2 fusion.148
  25.6 0.2 fusion.149
  25.8 0.1 fusion.150
  25.9 0.1 fusion.152
  26.0 0.1 collective-permute-start.2
  26.1 3.2 collective-permute-start.3
  29.3 2.3 collective-permute-done.2
  31.6 0.1 collective-permute-done.3
  31.7 0.8 fusion.73
  32.5 0.2 fusion.137
  32.6 0.2 fusion.138
  32.8 0.2 fusion.139
  33.0 0.2 fusion.140
  33.2 0.1 fusion.141
  33.3 0.1 fusion.143
  33.4 3.1 collective-permute-start.4
  36.5 0.5 collective-permute-start.5
  37.0 2.2 collective-permute-done.4
  39.2 0.1 collective-permute-done.5
  39.3 0.8 fusion.56
  40.0 0.2 fusion.128
  40.2 0.2 fusion.129
  40.4 0.2 fusion.130
  40.6 0.2 fusion.131
  40.8 0.1 fusion.132
  40.8 0.1 fusion.134
  40.9 3.1 collective-permute-start.6
  44.1 14.4 %collective-permute-start.7 = (f32[4,2,24,128]{3,2,1,0:T(8,128)S(1)}, f32[4,2,24,128]{3,2,1,0:T(8,128)S(1)}, u32[]{:S(2)}, u32[]{:S(2)}) collective-permute-start(f32[4,2,24,128]{3,2,1,0:T(8,128)S(1)} %get-tuple-element.45), channel_id=1, source_target_pairs={{1,0},{2,1},{3,2},{0,3},{5,4},{6,5},{7,6},{4,7},{9,8},{10,9},{11,1... | collective-permute-start | bytes 294920 | tf_op jit(solution)/shard_map/ppermute | solution.py:19
  58.5 2.2 collective-permute-done.7
  60.7 1.5 fusion.39
  62.2 1.0 fusion.127
  63.2 3.0 collective-permute-start.8
  66.2 0.5 collective-permute-start.9
  66.7 1.0 fusion.124
  67.7 1.3 fusion.119
  68.9 1.3 fusion.120
  70.2 1.3 fusion.121
  71.5 1.3 fusion.122
  72.8 1.2 fusion.123
  74.0 1.2 fusion.125
  75.2 1.0 fusion.126
  76.2 2.3 fusion.22
  78.5 534.0 %all-gather.2.cloned.1.call-done = f32[256,8,24,128]{3,2,1,0:T(8,128)} async-done(((f32[4,8,24,128]{3,2,1,0:T(8,128)}), f32[256,8,24,128]{3,2,1,0:T(8,128)}) %all-gather.2.cloned.1.call-update) | async-done | bytes 25165840 | tf_op jit(solution)/shard_map/all_gather | solution.py:50
  612.5 39.1 %fusion.4 = f32[4,256]{1,0:T(4,128)S(1)} fusion(f32[256,8,24,128]{3,2,1,0:T(8,128)} %all-gather.2.cloned.1.call-done, f32[4,8,24,128]{3,2,1,0:T(8,128)} %fusion.39), kind=kOutput, calls=%fused_computation.4 | convolution fusion | flops 301989888 | bytes 25563136 | tf_op jit(solution)/shard_map/dot_general | solution.py:52
  651.6 30.1 %fusion.7 = f32[4,256]{1,0:T(4,128)S(1)} fusion(f32[256,8,24,128]{3,2,1,0:T(8,128)} %all-gather.2.cloned.1.call-done, f32[4,8,24,128]{3,2,1,0:T(8,128)S(1)} %fusion.22), kind=kOutput, calls=%fused_computation.5 | convolution fusion | flops 301989888 | bytes 25563136 | tf_op jit(solution)/shard_map/dot_general | solution.py:55
  681.6 9.2 %all-reduce = (f32[4,256]{1,0:T(4,128)S(1)}, f32[4,256]{1,0:T(4,128)S(1)}) all-reduce(f32[4,256]{1,0:T(4,128)S(1)} %fusion.4, f32[4,256]{1,0:T(4,128)S(1)} %fusion.7), channel_id=1, replica_groups=mesh['band'=64,'slab'=4] {'slab'}, use_global_device_ids=true, to_apply=%region_0.1 | all-reduce | flops 2048 | bytes 16384 | tf_op jit(solution)/shard_map/psum | solution.py:58
  690.9 0.6 broadcast_multiply_fusion.2
  (21 shorter events, 0.3 us)
Async XLA Ops:
  7.2 24.5 %copy-start = (f32[4,8,24,128]{3,2,1,0:T(8,128)S(1)}, f32[4,8,24,128]{3,2,1,0:T(8,128)}, u32[]{:S(2)}) copy-start(f32[4,8,24,128]{3,2,1,0:T(8,128)} %param.2) | copy-start | bytes 1179652
  7.2 32.1 %copy-start.1 = (f32[8,24,128]{2,1,0:T(8,128)S(1)}, f32[8,24,128]{2,1,0:T(8,128)}, u32[]{:S(2)}) copy-start(f32[8,24,128]{2,1,0:T(8,128)} %param.3) | copy-start | bytes 294916
  7.2 605.3 %all-gather.2.cloned.1.call-start = ((), (), s32[]{:S(2)}) async-start(), calls=%async_computation | async-start | bytes 25559040 | tf_op jit(solution)/shard_map/all_gather | solution.py:50
  8.2 13.9 %collective-permute-start = (f32[4,2,24,128]{3,2,1,0:T(8,128)S(1)}, f32[4,2,24,128]{3,2,1,0:T(8,128)S(1)}, u32[]{:S(2)}, u32[]{:S(2)}) collective-permute-start(f32[4,2,24,128]{3,2,1,0:T(8,128)S(1)} %get-tuple-element.84), channel_id=1, source_target_pairs={{0,1},{1,2},{2,3},{3,0},{4,5},{5,6},{6,7},{7,4},{8,9},{9,10},{10,1... | collective-permute-start | bytes 294920 | tf_op jit(solution)/shard_map/ppermute | solution.py:16
  8.3 14.9 %collective-permute-start.1 = (f32[4,2,24,128]{3,2,1,0:T(8,128)S(1)}, f32[4,2,24,128]{3,2,1,0:T(8,128)S(1)}, u32[]{:S(2)}, u32[]{:S(2)}) collective-permute-start(f32[4,2,24,128]{3,2,1,0:T(8,128)S(1)} %get-tuple-element.85), channel_id=1, source_target_pairs={{1,0},{2,1},{3,2},{0,3},{5,4},{6,5},{7,6},{4,7},{9,8},{10,9},{11,1... | collective-permute-start | bytes 294920 | tf_op jit(solution)/shard_map/ppermute | solution.py:19
  26.0 5.6 collective-permute-start.2
  26.1 5.6 collective-permute-start.3
  33.4 5.8 collective-permute-start.4
  36.5 2.7 collective-permute-start.5
  40.9 17.6 %collective-permute-start.6 = (f32[4,2,24,128]{3,2,1,0:T(8,128)S(1)}, f32[4,2,24,128]{3,2,1,0:T(8,128)S(1)}, u32[]{:S(2)}, u32[]{:S(2)}) collective-permute-start(f32[4,2,24,128]{3,2,1,0:T(8,128)S(1)} %get-tuple-element.44), channel_id=1, source_target_pairs={{0,1},{1,2},{2,3},{3,0},{4,5},{5,6},{6,7},{7,4},{8,9},{9,10},{10,1... | collective-permute-start | bytes 294920 | tf_op jit(solution)/shard_map/ppermute | solution.py:16
  44.1 16.6 %collective-permute-start.7 = (f32[4,2,24,128]{3,2,1,0:T(8,128)S(1)}, f32[4,2,24,128]{3,2,1,0:T(8,128)S(1)}, u32[]{:S(2)}, u32[]{:S(2)}) collective-permute-start(f32[4,2,24,128]{3,2,1,0:T(8,128)S(1)} %get-tuple-element.45), channel_id=1, source_target_pairs={{1,0},{2,1},{3,2},{0,3},{5,4},{6,5},{7,6},{4,7},{9,8},{10,9},{11,1... | collective-permute-start | bytes 294920 | tf_op jit(solution)/shard_map/ppermute | solution.py:19
  63.2 13.0 %collective-permute-start.8 = (f32[4,2,24,128]{3,2,1,0:T(8,128)S(1)}, f32[4,2,24,128]{3,2,1,0:T(8,128)S(1)}, u32[]{:S(2)}, u32[]{:S(2)}) collective-permute-start(f32[4,2,24,128]{3,2,1,0:T(8,128)S(1)} %get-tuple-element.26), channel_id=1, source_target_pairs={{0,1},{1,2},{2,3},{3,0},{4,5},{5,6},{6,7},{7,4},{8,9},{9,10},{10,1... | collective-permute-start | bytes 294920 | tf_op jit(solution)/shard_map/ppermute | solution.py:16
  66.2 10.0 %collective-permute-start.9 = (f32[4,2,24,128]{3,2,1,0:T(8,128)S(1)}, f32[4,2,24,128]{3,2,1,0:T(8,128)S(1)}, u32[]{:S(2)}, u32[]{:S(2)}) collective-permute-start(f32[4,2,24,128]{3,2,1,0:T(8,128)S(1)} %get-tuple-element.27), channel_id=1, source_target_pairs={{1,0},{2,1},{3,2},{0,3},{5,4},{6,5},{7,6},{4,7},{9,8},{10,9},{11,1... | collective-permute-start | bytes 294920 | tf_op jit(solution)/shard_map/ppermute | solution.py:19
Sparse Core Ops, SparseCore 0:
  62.3 550.1 all-gather.1
where the time goes:
time: 707 us; the launch traced here: 699 us
  waiting for transfers between devices  541 us (77%)
  matrix products  69.1 us (10%)
  starting transfers between devices  31.3 us (4%)
  local copies, waits for them, and re-layouts  24.9 us (4%)
  between operations  14.7 us (2%)
  blocking collectives  9.23 us (1%)
  other arithmetic  8.61 us (1%)
    all_gather x1, waiting for transfers between devices, body(): piece = lax.all_gather(current, 'band', axis=0, tiled=True)  534 us
    dot_general x1, matrix products, body(): jnp.dot(flat, others.T, precision=lax.Precision.HIGHEST, preferred_elemen...  39.1 us
    dot_general x1, matrix products, body(): jnp.dot(himage, others.T, precision=lax.Precision.HIGHEST, preferred_elem...  30.1 us
    ppermute x5, starting transfers between devices, extended(): lax.ppermute(lax.slice_in_dim(block, 0, width, axis=dim), axis, backward)  21.8 us
  transfers between devices with their start and end apart: 11, of which 6 were waited for; matrix products, arithmetic and copies ran while one was open for 4% of the time, Pallas kernels for 0%

commit v1 on v0

--- a/solution.py
+++ b/solution.py
@@ -47,7 +47,8 @@
     volume = 1.0 / (current.shape[1] * lax.axis_size("slab") * current.shape[2] * current.shape[3])
     flat = current.reshape(local_bands, -1)
     himage = image.reshape(local_bands, -1)
-    piece = lax.all_gather(current, "band", axis=0, tiled=True)
+    sent = jnp.stack([current] * lax.axis_size("band"))
+    piece = jnp.concatenate(lax.all_to_all(sent, "band", 0, 0), axis=0)
     others = piece.reshape(piece.shape[0], -1)
     gram_part = jnp.dot(
         flat, others.T, precision=lax.Precision.HIGHEST, preferred_element_type=jnp.float32

time: 707 us -> 773 us (1.093)
  the two profiles are of different devices: /device:TPU:8 before, /device:TPU:100 now
where the time goes in v1:
time: 773 us; the launch traced here: 772 us
  waiting for transfers between devices  609 us (79%)
  local copies, waits for them, and re-layouts  50.1 us (6%)
  matrix products  45.4 us (6%)
  blocking collectives  41.9 us (5%)
  starting transfers between devices  18.2 us (2%)
    all_to_all x1, waiting for transfers between devices, body(): piece = jnp.concatenate(lax.all_to_all(sent, 'band', 0, 0), axis=0)  499 us
    ppermute x5, waiting for transfers between devices, extended(): lax.ppermute(lax.slice_in_dim(block, 0, width, axis=dim), axis, backward)  76.3 us
    psum x1, blocking collectives, body(): gram_total, proj_total = lax.psum((gram_part, proj_part), 'slab')  41.9 us
    ppermute x5, waiting for transfers between devices, extended(): lax.ppermute(lax.slice_in_dim(block, block.shape[dim] - width, None, axis...  33.8 us
    another operation x1, local copies, waits for them, and re-layouts, body(): others = piece.reshape(piece.shape[0], -1)  23.4 us
    dot_general x1, matrix products, body(): jnp.dot(himage, others.T, precision=lax.Precision.HIGHEST, preferred_elem...  22.7 us
    dot_general x1, matrix products, body(): jnp.dot(flat, others.T, precision=lax.Precision.HIGHEST, preferred_elemen...  22.7 us
  transfers between devices with their start and end apart: 11, of which 9 were waited for; matrix products, arithmetic and copies ran while one was open for 2% of the time, Pallas kernels for 0%

profile of v1, /device:TPU:100, one launch (start us, length us, event | category | flops | bytes accessed | tf_op | source)
XLA Modules:
  0.0 772.1 jit_solution(1925167266462359557)
XLA Ops:
  0.6 0.0 copy-start.1
  0.7 1.0 fusion.149
  1.7 0.1 collective-permute-start
  1.8 3.2 collective-permute-start.1
  5.0 1.3 fusion.156
  6.3 1.3 fusion.157
  7.6 1.3 fusion.154
  8.8 1.3 fusion.155
  10.1 1.0 fusion.152
  11.1 1.2 fusion.153
  12.3 1.2 fusion.151
  13.5 0.9 broadcast_multiply_fusion.1
  14.4 1.0 fusion.150
  15.4 1.1 constant_dynamic-update-slice_fusion
  16.5 1.8 broadcast_multiply_fusion
  18.3 0.1 fusion.146
  18.4 0.1 fusion.144
  18.4 0.2 fusion.142
  18.6 0.2 fusion.143
  18.8 0.2 fusion.140
  19.0 0.2 fusion.141
  19.2 0.1 collective-permute-start.3
  19.3 0.5 collective-permute-start.2
  19.8 2.6 collective-permute-done.3
  22.4 2.5 collective-permute-done.2
  24.9 0.8 fusion.63
  25.7 0.1 fusion.137
  25.8 0.1 fusion.135
  25.8 0.2 fusion.133
  26.0 0.2 fusion.134
  26.2 0.2 fusion.131
  26.4 0.2 fusion.132
  26.6 1.3 collective-permute-start.5
  27.9 3.0 collective-permute-done.5
  30.9 2.5 collective-permute-done.4
  33.5 0.8 fusion.46
  34.2 0.1 fusion.128
  34.3 0.1 fusion.126
  34.4 0.2 fusion.124
  34.6 0.2 fusion.125
  34.8 0.2 fusion.122
  35.0 0.2 fusion.123
  35.1 1.0 collective-permute-start.7
  36.2 3.2 collective-permute-done.7
  39.4 2.4 collective-permute-done.6
  41.7 0.7 fusion.29
  42.5 11.5 %stack.2 = f32[64,4,8,24,128]{4,3,2,1,0:T(8,128)} broadcast(f32[4,8,24,128]{3,2,1,0:T(8,128)S(1)} %fusion.29), dimensions={1,2,3,4} | broadcast | bytes 25559040 | tf_op jit(solution)/shard_map/stack | solution.py:50
  54.0 11.1 %all-to-all-start = ((f32[64,4,8,24,128]{4,3,2,1,0:T(8,128)}), f32[64,4,8,24,128]{4,3,2,1,0:T(8,128)}, u32[]{:S(2)}, u32[]{:S(2)}) async-start(f32[64,4,8,24,128]{4,3,2,1,0:T(8,128)} %stack.2), calls=%async_computation | async-start | bytes 50331648 | tf_op jit(solution)/shard_map/all_to_all | solution.py:51
  65.1 0.8 collective-permute-start.9
  65.9 0.1 fusion.119
  66.0 0.1 fusion.117
  66.1 0.2 fusion.115
  66.2 0.2 fusion.116
  66.4 0.2 fusion.113
  66.6 0.2 fusion.114
  66.8 67.5 %collective-permute-done.9 = f32[4,2,24,128]{3,2,1,0:T(8,128)S(1)} collective-permute-done((f32[4,2,24,128]{3,2,1,0:T(8,128)S(1)}, f32[4,2,24,128]{3,2,1,0:T(8,128)S(1)}, u32[]{:S(2)}, u32[]{:S(2)}) %collective-permute-start.9) | collective-permute-done | bytes 98336 | tf_op jit(solution)/shard_map/ppermute | solution.py:19
  134.3 26.5 %collective-permute-done.8 = f32[4,2,24,128]{3,2,1,0:T(8,128)S(1)} collective-permute-done((f32[4,2,24,128]{3,2,1,0:T(8,128)S(1)}, f32[4,2,24,128]{3,2,1,0:T(8,128)S(1)}, u32[]{:S(2)}, u32[]{:S(2)}) %collective-permute-start.8) | collective-permute-done | bytes 98336 | tf_op jit(solution)/shard_map/ppermute | solution.py:16
  160.8 0.7 fusion.12
  161.5 499.3 %all-to-all-done = f32[64,4,8,24,128]{4,3,2,1,0:T(8,128)} async-done(((f32[64,4,8,24,128]{4,3,2,1,0:T(8,128)}), f32[64,4,8,24,128]{4,3,2,1,0:T(8,128)}, u32[]{:S(2)}, u32[]{:S(2)}) %all-to-all-start) | async-done | bytes 25165856 | tf_op jit(solution)/shard_map/all_to_all | solution.py:51
  660.8 23.4 %reshape_reshape.3 = f32[256,24576]{1,0:T(8,128)} reshape(f32[64,4,8,24,128]{4,3,2,1,0:T(8,128)} %all-to-all-done) | data formatting | bytes 50331648 | tf_op jit(solution)/shard_map/reshape;reshape | solution.py:52
  684.2 22.7 %fusion.68 = f32[4,256]{1,0:T(4,128)S(1)} fusion(f32[256,24576]{1,0:T(8,128)} %reshape_reshape.3, f32[1,4,192,128]{3,2,1,0:T(8,128)S(1)} %bitcast.14), kind=kOutput, calls=%fused_computation.84 | convolution fusion | flops 301989888 | bytes 25563136 | tf_op jit(solution)/shard_map/dot_general | solution.py:53
  706.9 22.7 %fusion.65 = f32[4,256]{1,0:T(4,128)S(1)} fusion(f32[256,24576]{1,0:T(8,128)} %reshape_reshape.3, f32[1,4,192,128]{3,2,1,0:T(8,128)S(1)} %bitcast.15), kind=kOutput, calls=%fused_computation.81 | convolution fusion | flops 301989888 | bytes 25563136 | tf_op jit(solution)/shard_map/dot_general | solution.py:56
  729.6 41.9 %all-reduce = (f32[4,256]{1,0:T(4,128)S(1)}, f32[4,256]{1,0:T(4,128)S(1)}) all-reduce(f32[4,256]{1,0:T(4,128)S(1)} %fusion.68, f32[4,256]{1,0:T(4,128)S(1)} %fusion.65), channel_id=1, replica_groups=mesh['band'=64,'slab'=4] {'slab'}, use_global_device_ids=true, to_apply=%region_0.1 | all-reduce | flops 2048 | bytes 16384 | tf_op jit(solution)/shard_map/psum | solution.py:59
  771.5 0.6 broadcast_multiply_fusion.2
  (24 shorter events, 0.3 us)
Async XLA Ops:
  0.6 24.3 %copy-start.1 = (f32[4,8,24,128]{3,2,1,0:T(8,128)S(1)}, f32[4,8,24,128]{3,2,1,0:T(8,128)}, u32[]{:S(2)}) copy-start(f32[4,8,24,128]{3,2,1,0:T(8,128)} %param.2) | copy-start | bytes 1179652
  0.6 32.8 %copy-start.2 = (f32[8,24,128]{2,1,0:T(8,128)S(1)}, f32[8,24,128]{2,1,0:T(8,128)}, u32[]{:S(2)}) copy-start(f32[8,24,128]{2,1,0:T(8,128)} %param.3) | copy-start | bytes 294916
  1.7 13.7 %collective-permute-start = (f32[4,2,24,128]{3,2,1,0:T(8,128)S(1)}, f32[4,2,24,128]{3,2,1,0:T(8,128)S(1)}, u32[]{:S(2)}, u32[]{:S(2)}) collective-permute-start(f32[4,2,24,128]{3,2,1,0:T(8,128)S(1)} %get-tuple-element.81), channel_id=1, source_target_pairs={{0,1},{1,2},{2,3},{3,0},{4,5},{5,6},{6,7},{7,4},{8,9},{9,10},{10,1... | collective-permute-start | bytes 294920 | tf_op jit(solution)/shard_map/ppermute | solution.py:16
  1.8 14.7 %collective-permute-start.1 = (f32[4,2,24,128]{3,2,1,0:T(8,128)S(1)}, f32[4,2,24,128]{3,2,1,0:T(8,128)S(1)}, u32[]{:S(2)}, u32[]{:S(2)}) collective-permute-start(f32[4,2,24,128]{3,2,1,0:T(8,128)S(1)} %get-tuple-element.82), channel_id=1, source_target_pairs={{1,0},{2,1},{3,2},{0,3},{5,4},{6,5},{7,6},{4,7},{9,8},{10,9},{11,1... | collective-permute-start | bytes 294920 | tf_op jit(solution)/shard_map/ppermute | solution.py:19
  19.2 3.3 collective-permute-start.3
  19.3 5.6 collective-permute-start.2
  26.6 4.3 collective-permute-start.5
  27.9 5.5 collective-permute-start.4
  35.1 4.2 collective-permute-start.7
  36.2 5.5 collective-permute-start.6
  42.5 641.7 %copy-start = (f32[4,8,24,128]{3,2,1,0:T(8,128)}, f32[4,8,24,128]{3,2,1,0:T(8,128)S(1)}, u32[]{:S(2)}) copy-start(f32[4,8,24,128]{3,2,1,0:T(8,128)S(1)} %fusion.29) | copy-start | bytes 1179652
  54.0 606.8 %all-to-all-start = ((f32[64,4,8,24,128]{4,3,2,1,0:T(8,128)}), f32[64,4,8,24,128]{4,3,2,1,0:T(8,128)}, u32[]{:S(2)}, u32[]{:S(2)}) async-start(f32[64,4,8,24,128]{4,3,2,1,0:T(8,128)} %stack.2), calls=%async_computation | async-start | bytes 50331648 | tf_op jit(solution)/shard_map/all_to_all | solution.py:51
  65.1 69.3 %collective-permute-start.9 = (f32[4,2,24,128]{3,2,1,0:T(8,128)S(1)}, f32[4,2,24,128]{3,2,1,0:T(8,128)S(1)}, u32[]{:S(2)}, u32[]{:S(2)}) collective-permute-start(f32[4,2,24,128]{3,2,1,0:T(8,128)S(1)} %get-tuple-element.24), channel_id=1, source_target_pairs={{1,0},{2,1},{3,2},{0,3},{5,4},{6,5},{7,6},{4,7},{9,8},{10,9},{11,1... | collective-permute-start | bytes 294920 | tf_op jit(solution)/shard_map/ppermute | solution.py:19
  65.9 94.9 %collective-permute-start.8 = (f32[4,2,24,128]{3,2,1,0:T(8,128)S(1)}, f32[4,2,24,128]{3,2,1,0:T(8,128)S(1)}, u32[]{:S(2)}, u32[]{:S(2)}) collective-permute-start(f32[4,2,24,128]{3,2,1,0:T(8,128)S(1)} %get-tuple-element.23), channel_id=1, source_target_pairs={{0,1},{1,2},{2,3},{3,0},{4,5},{5,6},{6,7},{7,4},{8,9},{9,10},{10,1... | collective-permute-start | bytes 294920 | tf_op jit(solution)/shard_map/ppermute | solution.py:16
